TPU v7x, 128 devices: a whole 4x4x4 slice. The times are simulated.
128 devices in a mesh: prow: 8 (over y_lo, x), pcol: 16 (over y_hi, z, core).
Axes of the slice: x: 4, y: 4 (y_hi: 2, y_lo: 2; y = y_hi * 2 + y_lo), z: 4, core: 2. Of those that a mesh axis runs over, the one named last changes fastest.
Arguments:
- l_panel: bfloat16 [16384, 2048], P('prow', 'pcol'), may hold values from -0.29882812 to 0.29882812
- inverse_tile: bfloat16 [16384, 16384], P('prow', 'pcol'), may hold values from -0.375 to 0.375
- unit_inverse: bfloat16 [16, 128, 128], P('pcol'), may hold values from -0.5 to 0.5
- pivot_inverse: float32 [16, 128, 128], P('pcol'), may hold values from -6 to 6
- listed: int32 [16, 128], replicated, may hold values 0 or 1
Outputs:
- offdiag: float32 [2048, 16384], P('pcol', 'prow')
- diag: float32 [16, 128, 128], P('pcol')
All inputs are finite; a program needn't handle non-finite values.
Results may differ from a plain program's by a relative error of at most 0.015.
Values may be sent and summed in bfloat16 or wider, within the bound.
A program may use at most 64 MiB of HBM per device.

v0:
```python
import jax
import jax.numpy as jnp
from jax import lax
from jax.sharding import PartitionSpec as P

BLOCK = 128


def broadcast(block, axis, source):
    block = jnp.where(lax.axis_index(axis) == source, block, jnp.zeros_like(block))
    return lax.psum(block, axis)


def per_device(l_panel, inverse_tile, unit_inverse, pivot_inverse, listed):
    rows = l_panel.shape[0]
    columns = inverse_tile.shape[1]
    count_sn = unit_inverse.shape[0]
    width = unit_inverse.shape[1]
    row_index = lax.axis_index("prow")
    col_index = lax.axis_index("pcol")
    blocks = rows // BLOCK
    mine = lax.dynamic_slice(listed, (col_index * count_sn, row_index * blocks), (count_sn, blocks))
    row_mask = jnp.repeat(mine, BLOCK, axis=1).astype(jnp.bfloat16)
    masked = l_panel.reshape(rows, count_sn, width) * row_mask.T[:, :, None]
    lhat = jnp.einsum(
        "nsw,swv->nsv", masked, unit_inverse, preferred_element_type=jnp.float32
    ).astype(jnp.bfloat16)
    lhat_flat = lhat.reshape(rows, count_sn * width)
    ratio = lax.axis_size("pcol") // lax.axis_size("prow")
    wide_rows = lax.all_gather(lhat_flat, "pcol", axis=1, tiled=True)
    source = broadcast(wide_rows, "prow", col_index // ratio)
    mirrored = lax.dynamic_slice_in_dim(source, col_index % ratio * columns, columns, 0)
    product_t = lax.psum_scatter(
        lax.dot_general(
            mirrored, inverse_tile, (((0,), (1,)), ((), ())), preferred_element_type=jnp.float32
        ).astype(jnp.bfloat16),
        "pcol",
        scatter_dimension=0,
        tiled=True,
    ).astype(jnp.float32)
    wide_mask = jnp.repeat(row_mask.astype(jnp.float32), width, axis=0)
    offdiag = -(product_t * wide_mask)
    stacked = product_t.reshape(count_sn, width, rows)
    partial_diag = jnp.einsum(
        "svn,nsw->svw", stacked, lhat.astype(jnp.float32), precision=lax.Precision.HIGHEST
    )
    total = lax.psum(partial_diag.astype(jnp.bfloat16), "prow").astype(jnp.float32)
    diag = pivot_inverse + total
    return (offdiag, diag)


def solution(mesh):
    return jax.shard_map(
        per_device,
        mesh=mesh,
        in_specs=(
            P("prow", "pcol"),
            P("prow", "pcol"),
            P("pcol", None, None),
            P("pcol", None, None),
            P(),
        ),
        out_specs=(P("pcol", "prow"), P("pcol", None, None)),
        check_vma=False,
    )
```

profile of v0, /device:TPU:0, one launch (start us, length us, event | category | flops | bytes accessed | tf_op | source)
XLA Modules:
  0.0 439.2 jit_solution(7294961271793885270)
XLA Ops:
  7.2 0.0 copy-start
  7.2 0.0 all-gather.2.cloned.1.call-start
  7.2 0.8 convert_bitcast_fusion
  8.0 0.1 bitcast_convert_fusion
  8.1 0.0 copy-done
  8.1 2.3 convolution_convert_fusion.1
  10.4 0.0 all-gather.2.cloned.1.call-update
  10.4 0.0 all-reduce.2.cloned.1.call-start
  10.5 80.2 %all-gather.2.cloned.1.call-done = bf16[2048,2048]{1,0:T(8,128)(2,1)} async-done(((bf16[2048,128]{1,0:T(8,128)(2,1)}), bf16[2048,2048]{1,0:T(8,128)(2,1)}) %all-gather.2.cloned.1.call-update) | async-done | bytes 8388624 | tf_op jit(solution)/shard_map/all_gather | solution.py:30
  90.6 7.1 %broadcast_select_fusion = bf16[2048,2048]{1,0:T(8,128)(2,1)} fusion(bf16[2048,2048]{1,0:T(8,128)(2,1)} %all-gather.2.cloned.1.call-done, pred[]{:T(512)S(6)} %eq.5), kind=kLoop, calls=%fused_computation | loop fusion | flops 4194304 | bytes 16777216 | tf_op jit(solution)/shard_map/jit(_where)/select_n | solution.py:10
  97.8 0.0 all-reduce.2.cloned.1.call-update
  97.8 0.0 reduce-scatter.2.cloned.1.call-start
  97.9 181.8 %all-reduce.2.cloned.1.call-done = bf16[2048,2048]{1,0:T(8,128)(2,1)} async-done(((bf16[2048,2048]{1,0:T(8,128)(2,1)}), bf16[2048,2048]{1,0:T(8,128)(2,1)}) %all-reduce.2.cloned.1.call-update) | async-done | bytes 8388624 | tf_op jit(solution)/shard_map/psum | solution.py:11
  279.6 14.0 %convolution_convert_fusion = bf16[2048,2048]{1,0:T(8,128)(2,1)} fusion(bf16[2048,1024]{1,0:T(8,128)(2,1)} %param.6, bf16[2048,2048]{1,0:T(8,128)(2,1)} %all-reduce.2.cloned.1.call-done, s32[]{:T(128)S(6)} %select_n.34), kind=kOutput, calls=%fused_computation.1 | convolution fusion | flops 8594128896 | bytes 16777220 | tf_op jit(solution)/shard_map/dot_general | solution.py:34
  293.6 0.0 copy-start.1
  293.6 0.0 copy-start.2
  293.6 0.0 reduce-scatter.2.cloned.1.call-update
  293.7 101.6 %reduce-scatter.2.cloned.1.call-done = bf16[128,2048]{1,0:T(8,128)(2,1)} async-done(((bf16[2048,2048]{1,0:T(8,128)(2,1)}), bf16[128,2048]{1,0:T(8,128)(2,1)}) %reduce-scatter.2.cloned.1.call-update) | async-done | bytes 524304 | tf_op jit(solution)/shard_map/reduce_scatter | solution.py:33
  395.2 0.0 copy-done.1
  395.2 1.3 fusion.1
  396.6 33.3 %psum.15 = bf16[1,128,128]{2,1,0:T(8,128)(2,1)S(1)} all-reduce(bf16[1,128,128]{2,1,0:T(8,128)(2,1)S(1)} %fusion.1), channel_id=1, replica_groups=mesh['prow'=8,'pcol'=16] {'prow'}, use_global_device_ids=true, to_apply=%region_2.3 | all-reduce | flops 16384 | bytes 65536 | tf_op jit(solution)/shard_map/psum | solution.py:47
  429.9 0.0 copy-done.2
  429.9 0.6 convert_add_fusion
  430.5 2.2 multiply_negate_fusion
Async XLA Ops:
  7.2 0.9 copy-start
  7.2 83.4 %all-gather.2.cloned.1.call-start = ((), (), s32[]{:S(2)}) async-start(), calls=%async_computation.1 | async-start | bytes 8912896 | tf_op jit(solution)/shard_map/all_gather | solution.py:30
  10.4 269.2 %all-reduce.2.cloned.1.call-start = ((), (), s32[]{:S(2)}) async-start(), calls=%async_computation.2 | async-start | bytes 16777216 | tf_op jit(solution)/shard_map/psum | solution.py:11
  97.8 297.4 %reduce-scatter.2.cloned.1.call-start = ((), (), s32[]{:S(2)}) async-start(), calls=%async_computation.3 | async-start | bytes 8912896 | tf_op jit(solution)/shard_map/reduce_scatter | solution.py:33
  293.6 101.6 %copy-start.1 = (bf16[2048,128]{1,0:T(8,128)(2,1)S(1)}, bf16[2048,128]{1,0:T(8,128)(2,1)}, u32[]{:S(2)}) copy-start(bf16[2048,128]{1,0:T(8,128)(2,1)} %convolution_convert_fusion.1) | copy-start | bytes 1572868
  293.6 136.2 %copy-start.2 = (f32[1,128,128]{2,1,0:T(8,128)S(1)}, f32[1,128,128]{2,1,0:T(8,128)}, u32[]{:S(2)}) copy-start(f32[1,128,128]{2,1,0:T(8,128)} %param.8) | copy-start | bytes 196612
Sparse Core Ops, SparseCore 0:
  10.9 79.7 all-gather.1
  97.9 181.6 all-reduce.1
  293.8 101.3 reduce-scatter.1
where the time goes:
time: 440 us; the launch traced here: 439 us
  waiting for transfers between devices  364 us (83%)
  blocking collectives  33.3 us (8%)
  matrix products  17.7 us (4%)
  between operations  13.8 us (3%)
  other arithmetic  10.8 us (2%)
    psum x1, waiting for transfers between devices, broadcast(): return lax.psum(block, axis)  182 us
    reduce_scatter x1, waiting for transfers between devices, per_device(): lax.psum_scatter(lax.dot_general(mirrored, inverse_tile, (((0,), (1,)), (...  102 us
    all_gather x1, waiting for transfers between devices, per_device(): wide_rows = lax.all_gather(lhat_flat, 'pcol', axis=1, tiled=True)  80.2 us
    psum x1, blocking collectives, per_device(): lax.psum(partial_diag.astype(jnp.bfloat16), 'prow').astype(jnp.float32)  33.3 us
    dot_general x1, matrix products, per_device(): lax.dot_general(mirrored, inverse_tile, (((0,), (1,)), ((), ())), preferr...  14 us
  transfers between devices with their start and end apart: 3, of which 3 were waited for; matrix products, arithmetic and copies ran while one was open for 0% of the time, Pallas kernels for 0%

commit v1 on v0

--- a/solution.py
+++ b/solution.py
@@ -44,7 +44,9 @@
     partial_diag = jnp.einsum(
         "svn,nsw->svw", stacked, lhat.astype(jnp.float32), precision=lax.Precision.HIGHEST
     )
-    total = lax.psum(partial_diag.astype(jnp.bfloat16), "prow").astype(jnp.float32)
+    total = jnp.sum(lax.all_gather(partial_diag.astype(jnp.bfloat16), "prow"), axis=0).astype(
+        jnp.float32
+    )
     diag = pivot_inverse + total
     return (offdiag, diag)
 

time: 440 us -> 435 us (0.989)
  blocking collectives: 33.3 us -> 28.4 us
    psum x1 -> x0, blocking collectives: 33.3 us -> none  [per_device(): lax.psum(partial_diag.astype(jnp.bfloat16), 'prow').astype(jnp.float32)]
    all_gather x0 -> x1, blocking collectives: none -> 28.4 us  [per_device(): lax.all_gather(partial_diag.astype(jnp.bfloat16), 'prow')]
where the time goes in v1:
time: 435 us; the launch traced here: 434 us
  waiting for transfers between devices  364 us (84%)
  blocking collectives  28.4 us (7%)
  matrix products  17.7 us (4%)
  between operations  13.8 us (3%)
  other arithmetic  10.8 us (2%)
    psum x1, waiting for transfers between devices, broadcast(): return lax.psum(block, axis)  182 us
    reduce_scatter x1, waiting for transfers between devices, per_device(): lax.psum_scatter(lax.dot_general(mirrored, inverse_tile, (((0,), (1,)), (...  102 us
    all_gather x1, waiting for transfers between devices, per_device(): wide_rows = lax.all_gather(lhat_flat, 'pcol', axis=1, tiled=True)  80.2 us
    all_gather x1, blocking collectives, per_device(): lax.all_gather(partial_diag.astype(jnp.bfloat16), 'prow')  28.4 us
    dot_general x1, matrix products, per_device(): lax.dot_general(mirrored, inverse_tile, (((0,), (1,)), ((), ())), preferr...  14 us
  transfers between devices with their start and end apart: 3, of which 3 were waited for; matrix products, arithmetic and copies ran while one was open for 0% of the time, Pallas kernels for 0%

profile of v1, /device:TPU:0, one launch (start us, length us, event | category | flops | bytes accessed | tf_op | source)
XLA Modules:
  0.0 434.3 jit_solution(16175819663809444658)
XLA Ops:
  7.2 0.0 copy-start
  7.2 0.0 all-gather.3.cloned.1.call-start
  7.2 0.8 convert_bitcast_fusion
  8.0 0.1 bitcast_convert_fusion
  8.1 0.0 copy-done
  8.1 2.3 convolution_convert_fusion.1
  10.4 0.0 all-gather.3.cloned.1.call-update
  10.4 0.0 all-reduce.2.cloned.1.call-start
  10.5 80.2 %all-gather.3.cloned.1.call-done = bf16[2048,2048]{1,0:T(8,128)(2,1)} async-done(((bf16[2048,128]{1,0:T(8,128)(2,1)}), bf16[2048,2048]{1,0:T(8,128)(2,1)}) %all-gather.3.cloned.1.call-update) | async-done | bytes 8388624 | tf_op jit(solution)/shard_map/all_gather | solution.py:30
  90.6 7.1 %broadcast_select_fusion = bf16[2048,2048]{1,0:T(8,128)(2,1)} fusion(bf16[2048,2048]{1,0:T(8,128)(2,1)} %all-gather.3.cloned.1.call-done, pred[]{:T(512)S(6)} %eq.5), kind=kLoop, calls=%fused_computation | loop fusion | flops 4194304 | bytes 16777216 | tf_op jit(solution)/shard_map/jit(_where)/select_n | solution.py:10
  97.8 0.0 all-reduce.2.cloned.1.call-update
  97.8 0.0 reduce-scatter.2.cloned.1.call-start
  97.9 181.8 %all-reduce.2.cloned.1.call-done = bf16[2048,2048]{1,0:T(8,128)(2,1)} async-done(((bf16[2048,2048]{1,0:T(8,128)(2,1)}), bf16[2048,2048]{1,0:T(8,128)(2,1)}) %all-reduce.2.cloned.1.call-update) | async-done | bytes 8388624 | tf_op jit(solution)/shard_map/psum | solution.py:11
  279.6 14.0 %convolution_convert_fusion = bf16[2048,2048]{1,0:T(8,128)(2,1)} fusion(bf16[2048,1024]{1,0:T(8,128)(2,1)} %param.6, bf16[2048,2048]{1,0:T(8,128)(2,1)} %all-reduce.2.cloned.1.call-done, s32[]{:T(128)S(6)} %select_n.34), kind=kOutput, calls=%fused_computation.1 | convolution fusion | flops 8594128896 | bytes 16777220 | tf_op jit(solution)/shard_map/dot_general | solution.py:34
  293.6 0.0 copy-start.1
  293.6 0.0 copy-start.2
  293.6 0.0 reduce-scatter.2.cloned.1.call-update
  293.7 101.6 %reduce-scatter.2.cloned.1.call-done = bf16[128,2048]{1,0:T(8,128)(2,1)} async-done(((bf16[2048,2048]{1,0:T(8,128)(2,1)}), bf16[128,2048]{1,0:T(8,128)(2,1)}) %reduce-scatter.2.cloned.1.call-update) | async-done | bytes 524304 | tf_op jit(solution)/shard_map/reduce_scatter | solution.py:33
  395.2 0.0 copy-done.1
  395.2 1.3 convolution_convert_fusion.2
  396.6 28.4 %all-gather = bf16[1024,128]{1,0:T(8,128)(2,1)S(1)} all-gather(bf16[128,128]{1,0:T(8,128)(2,1)S(1)} %convolution_convert_fusion.2), channel_id=2, replica_groups=mesh['prow'=8,'pcol'=16] {'prow'}, dimensions={0}, use_global_device_ids=true | all-gather | bytes 294912 | tf_op jit(solution)/shard_map/all_gather | solution.py:47
  425.0 0.0 copy-done.2
  425.0 0.6 convert_add_fusion
  425.7 2.2 multiply_negate_fusion
  (1 shorter events, 0.0 us)
Async XLA Ops:
  7.2 0.9 copy-start
  7.2 83.4 %all-gather.3.cloned.1.call-start = ((), (), s32[]{:S(2)}) async-start(), calls=%async_computation.1 | async-start | bytes 8912896 | tf_op jit(solution)/shard_map/all_gather | solution.py:30
  10.4 269.2 %all-reduce.2.cloned.1.call-start = ((), (), s32[]{:S(2)}) async-start(), calls=%async_computation.2 | async-start | bytes 16777216 | tf_op jit(solution)/shard_map/psum | solution.py:11
  97.8 297.4 %reduce-scatter.2.cloned.1.call-start = ((), (), s32[]{:S(2)}) async-start(), calls=%async_computation.3 | async-start | bytes 8912896 | tf_op jit(solution)/shard_map/reduce_scatter | solution.py:33
  293.6 101.6 %copy-start.1 = (bf16[2048,128]{1,0:T(8,128)(2,1)S(1)}, bf16[2048,128]{1,0:T(8,128)(2,1)}, u32[]{:S(2)}) copy-start(bf16[2048,128]{1,0:T(8,128)(2,1)} %convolution_convert_fusion.1) | copy-start | bytes 1572868
  293.6 131.4 %copy-start.2 = (f32[1,128,128]{2,1,0:T(8,128)S(1)}, f32[1,128,128]{2,1,0:T(8,128)}, u32[]{:S(2)}) copy-start(f32[1,128,128]{2,1,0:T(8,128)} %param.8) | copy-start | bytes 196612
Sparse Core Ops, SparseCore 0:
  10.9 79.7 all-gather.2
  97.9 181.6 all-reduce.1
  293.8 101.3 reduce-scatter.1
